TPU v7x, 32 devices: a whole 2x2x4 slice. The times are simulated.
32 devices in a mesh: seq: 8 (over z, y), head: 4 (over x, core).
Axes of the slice: x: 2, y: 2, z: 4, core: 2. Of those that a mesh axis runs over, the one named last changes fastest.
Arguments:
- queries: bfloat16 [8192, 512], P(('seq', 'head')), may hold values from -6 to 6
- key_rows: bfloat16 [8192, 128], P(('seq', 'head')), may hold values from -6 to 6
- value_rows: bfloat16 [8192, 128], P(('seq', 'head')), may hold values from -6 to 6
- out_grad: bfloat16 [8192, 512], P(('seq', 'head')), may hold values from -6 to 6
- doc_start: int32 [32], replicated, may hold values from 0 to 255
Outputs:
- outputs: bfloat16 [8192, 512], P(('seq', 'head'))
- query_grad: bfloat16 [8192, 512], P(('seq', 'head'))
- key_grad: bfloat16 [8192, 128], P(('seq', 'head'))
- value_grad: bfloat16 [8192, 128], P(('seq', 'head'))
Inputs may be any that keep to these rules, and one draw needn't show every extreme that they name: doc_start[c] is the position within span c of the first token of a new document.
All inputs are finite; a program needn't handle non-finite values.
Results may differ from a plain program's by a relative error of at most 0.0065.
Values may be sent and summed in bfloat16 or wider, within the bound.
No kernel may reach another device: no remote copies, remote signals or barrier semaphores. Data moves between devices by JAX's collectives and lax.ppermute only.
A program may use at most 128 MiB of HBM per device.

v0:
```python
import math

import jax
import jax.numpy as jnp
from jax import lax
from jax.sharding import PartitionSpec as P

HD = 128
GROUP = 4
SPANS_DEV = 4


masked_fill = -1e30


def passed_along(value, axis, steps):
    count = lax.axis_size(axis)
    first, last = (max(0, -steps), min(count, count - steps))
    return lax.ppermute(value, axis, [(source, source + steps) for source in range(first, last)])


def allowed_mask(
    first_row, row_count, key_count, halo_len, span_len, span_start, prev_begin, span_index
):
    row_pos = first_row + lax.broadcasted_iota(jnp.int32, (row_count, key_count), 0)
    col_pos = lax.broadcasted_iota(jnp.int32, (row_count, key_count), 1) - halo_len
    return (
        (col_pos <= row_pos)
        & ((col_pos >= span_start) | (span_start > row_pos))
        & (col_pos >= prev_begin - span_len)
        & ((col_pos >= 0) | (span_index > 0))
    )


def attend(query_rows, grad_rows, key_block, value_block, allowed, head_dim):
    score_scale = 1.0 / math.sqrt(head_dim)
    contract = (((2,), (2,)), ((0,), (0,)))
    forward = (((2,), (1,)), ((0,), (0,)))
    backward = (((1,), (1,)), ((0,), (0,)))
    scores = (
        lax.dot_general(query_rows, key_block, contract, preferred_element_type=jnp.float32)
        * score_scale
    )
    masked = jnp.where(allowed, scores, masked_fill)
    row_max = jnp.max(masked, axis=2, keepdims=True)
    exp_scores = jnp.where(allowed, jnp.exp(masked - row_max), 0.0)
    weights = exp_scores / jnp.sum(exp_scores, axis=2, keepdims=True)
    weights_low = weights.astype(jnp.bfloat16)
    result = lax.dot_general(
        weights_low, value_block, forward, preferred_element_type=jnp.float32
    ).astype(jnp.bfloat16)
    grad_weights = lax.dot_general(
        grad_rows, value_block, contract, preferred_element_type=jnp.float32
    )
    row_delta = jnp.sum(weights * grad_weights, axis=2, keepdims=True)
    grad_scores = (weights * (grad_weights - row_delta) * score_scale).astype(jnp.bfloat16)
    grad_query = lax.dot_general(
        grad_scores, key_block, forward, preferred_element_type=jnp.float32
    )
    grad_key = lax.dot_general(
        grad_scores, query_rows, backward, preferred_element_type=jnp.float32
    )
    grad_value = lax.dot_general(
        weights_low, grad_rows, backward, preferred_element_type=jnp.float32
    )
    return (result, grad_query, grad_key, grad_value)


def per_device(queries, key_rows, value_rows, out_grad, doc_start):
    tok_count = queries.shape[0]
    head_count = lax.axis_size("head")
    group_rows = tok_count * head_count
    span_len = group_rows // SPANS_DEV
    halo_len = span_len // 4
    half_len = span_len // 2
    rest_len = span_len - halo_len
    head_q, head_grad = (
        lax.all_to_all(queries, "head", split_axis=1, concat_axis=0, tiled=True),
        lax.all_to_all(out_grad, "head", split_axis=1, concat_axis=0, tiled=True),
    )
    full_k, full_v = (
        lax.all_gather(key_rows, "head", axis=0, tiled=True),
        lax.all_gather(value_rows, "head", axis=0, tiled=True),
    )
    column = lax.axis_index("head") // GROUP * HD
    head_k = lax.dynamic_slice_in_dim(full_k, column, HD, 1)
    head_v = lax.dynamic_slice_in_dim(full_v, column, HD, 1)
    query_3 = head_q.reshape(SPANS_DEV, span_len, HD)
    grad_3 = head_grad.reshape(SPANS_DEV, span_len, HD)
    keys_3 = head_k.reshape(SPANS_DEV, span_len, HD)
    values_3 = head_v.reshape(SPANS_DEV, span_len, HD)
    tail_k = keys_3[:, rest_len:]
    tail_v = values_3[:, rest_len:]
    edge_last_k, edge_last_v = passed_along(
        (tail_k[SPANS_DEV - 1], tail_v[SPANS_DEV - 1]), "seq", 1
    )
    edge_k = jnp.concatenate([edge_last_k[None], tail_k[: SPANS_DEV - 1]], axis=0)
    edge_v = jnp.concatenate([edge_last_v[None], tail_v[: SPANS_DEV - 1]], axis=0)
    key_block = jnp.concatenate([edge_k, keys_3], axis=1)
    value_block = jnp.concatenate([edge_v, values_3], axis=1)
    first_span = lax.axis_index("seq") * SPANS_DEV
    span_starts = lax.dynamic_slice_in_dim(doc_start, first_span, SPANS_DEV)
    before_start = lax.dynamic_slice_in_dim(doc_start, jnp.maximum(first_span - 1, 0), 1)
    prev_starts = jnp.concatenate([before_start, span_starts[: SPANS_DEV - 1]], axis=0)
    span_ids = first_span + jnp.arange(SPANS_DEV, dtype=jnp.int32)
    span_starts = span_starts.reshape(SPANS_DEV, 1, 1)
    prev_starts = prev_starts.reshape(SPANS_DEV, 1, 1)
    span_ids = span_ids.reshape(SPANS_DEV, 1, 1)
    grad_key = jnp.zeros((SPANS_DEV, halo_len + span_len, HD), jnp.float32)
    grad_value = jnp.zeros((SPANS_DEV, halo_len + span_len, HD), jnp.float32)
    results = []
    query_grads = []
    for block_index in range(2):
        first_row = block_index * half_len
        key_count = halo_len + first_row + half_len
        allowed = allowed_mask(
            first_row, half_len, key_count, halo_len, span_len, span_starts, prev_starts, span_ids
        )
        result, grad_query, part_key, part_value = attend(
            query_3[:, first_row : first_row + half_len],
            grad_3[:, first_row : first_row + half_len],
            key_block[:, :key_count],
            value_block[:, :key_count],
            allowed,
            HD,
        )
        results.append(result)
        query_grads.append(grad_query.astype(jnp.bfloat16))
        grad_key = grad_key.at[:, :key_count].add(part_key)
        grad_value = grad_value.at[:, :key_count].add(part_value)
    next_last_k, next_last_v = passed_along(
        (grad_key[0, :halo_len], grad_value[0, :halo_len]), "seq", -1
    )
    next_k = jnp.concatenate([grad_key[1:, :halo_len], next_last_k[None]], axis=0)
    next_v = jnp.concatenate([grad_value[1:, :halo_len], next_last_v[None]], axis=0)
    own_k = jnp.concatenate(
        [grad_key[:, halo_len : halo_len + rest_len], grad_key[:, halo_len + rest_len :] + next_k],
        axis=1,
    ).reshape(group_rows, HD)
    own_v = jnp.concatenate(
        [
            grad_value[:, halo_len : halo_len + rest_len],
            grad_value[:, halo_len + rest_len :] + next_v,
        ],
        axis=1,
    ).reshape(group_rows, HD)
    all_results = jnp.concatenate(results, axis=1).reshape(group_rows, HD)
    all_query_grads = jnp.concatenate(query_grads, axis=1).reshape(group_rows, HD)
    outputs, query_grad = (
        lax.all_to_all(all_results, "head", split_axis=0, concat_axis=1, tiled=True),
        lax.all_to_all(all_query_grads, "head", split_axis=0, concat_axis=1, tiled=True),
    )
    wide_gk, wide_gv = (
        lax.all_to_all(own_k, "head", split_axis=0, concat_axis=1, tiled=True),
        lax.all_to_all(own_v, "head", split_axis=0, concat_axis=1, tiled=True),
    )
    group_total = wide_gk.shape[1] // (GROUP * HD)
    key_grad = (
        wide_gk.reshape(tok_count, group_total, GROUP, HD)
        .sum(axis=2)
        .reshape(tok_count, group_total * HD)
        .astype(jnp.bfloat16)
    )
    value_grad = (
        wide_gv.reshape(tok_count, group_total, GROUP, HD)
        .sum(axis=2)
        .reshape(tok_count, group_total * HD)
        .astype(jnp.bfloat16)
    )
    return (outputs, query_grad, key_grad, value_grad)


def solution(mesh):
    placed = (
        P(("seq", "head"), None),
        P(("seq", "head"), None),
        P(("seq", "head"), None),
        P(("seq", "head"), None),
        P(),
    )
    return jax.shard_map(
        per_device,
        mesh=mesh,
        in_specs=placed,
        out_specs=(
            P(("seq", "head"), None),
            P(("seq", "head"), None),
            P(("seq", "head"), None),
            P(("seq", "head"), None),
        ),
        check_vma=False,
    )
```

profile of v0, /device:TPU:8, one launch (start us, length us, event | category | flops | bytes accessed | tf_op | source)
XLA Modules:
  0.0 94.2 jit_solution(2533710951645964501)
XLA Ops:
  0.6 6.1 %all_gather.7 = bf16[1024,128]{1,0:T(8,128)(2,1)S(1)} all-gather(bf16[256,128]{1,0:T(8,128)(2,1)} %param.19), channel_id=1, replica_groups=mesh['seq'=8,'head'=4] {'head'}, dimensions={0}, use_global_device_ids=true | all-gather | bytes 327680 | tf_op jit(solution)/shard_map/all_gather | solution.py:83
  6.8 3.5 %collective-permute-start.1 = (bf16[64,128]{1,0:T(8,128)(2,1)S(1)}, bf16[64,128]{1,0:T(8,128)(2,1)S(1)}, u32[]{:S(2)}, u32[]{:S(2)}) collective-permute-start(bf16[64,128]{1,0:T(8,128)(2,1)S(1)} %slice_bitcast_fusion.2), channel_id=1, source_target_pairs={{0,4},{4,8},{8,12},{12,16},{16,20},{20,24},{24,28},{1,5},{5,9},{9,... | collective-permute-start | bytes 49160 | tf_op jit(solution)/shard_map/ppermute | solution.py:19
  10.3 5.8 %all_gather.6 = bf16[1024,128]{1,0:T(8,128)(2,1)S(1)} all-gather(bf16[256,128]{1,0:T(8,128)(2,1)S(1)} %copy-done.2), channel_id=1, replica_groups=mesh['seq'=8,'head'=4] {'head'}, dimensions={0}, use_global_device_ids=true | all-gather | bytes 327680 | tf_op jit(solution)/shard_map/all_gather | solution.py:82
  16.1 3.4 %collective-permute-start = (bf16[64,128]{1,0:T(8,128)(2,1)S(1)}, bf16[64,128]{1,0:T(8,128)(2,1)S(1)}, u32[]{:S(2)}, u32[]{:S(2)}) collective-permute-start(bf16[64,128]{1,0:T(8,128)(2,1)S(1)} %slice_bitcast_fusion.3), channel_id=1, source_target_pairs={{0,4},{4,8},{8,12},{12,16},{16,20},{20,24},{24,28},{1,5},{5,9},{9,... | collective-permute-start | bytes 49160 | tf_op jit(solution)/shard_map/ppermute | solution.py:19
  19.6 0.1 copy.12
  19.7 0.8 copy.13
  20.6 3.5 %all-to-all-start.2 = ((bf16[256,4,128]{2,0,1:T(8,128)(2,1)}), bf16[256,4,128]{2,0,1:T(8,128)(2,1)S(1)}, u32[]{:S(2)}, u32[]{:S(2)}) async-start(bf16[256,4,128]{2,0,1:T(8,128)(2,1)} %copy.13), calls=%async_computation.2 | async-start | bytes 524288 | tf_op jit(solution)/shard_map/all_to_all | solution.py:79
  24.3 0.6 dynamic_slice.9
  24.9 0.1 iota_compare_fusion.1
  25.0 0.1 broadcast_compare_fusion
  25.1 0.7 add_add_fusion
  25.9 0.1 copy.9
  26.0 0.8 copy.10
  26.9 3.2 %all-to-all-done.2 = bf16[256,4,128]{2,0,1:T(8,128)(2,1)S(1)} async-done(((bf16[256,4,128]{2,0,1:T(8,128)(2,1)}), bf16[256,4,128]{2,0,1:T(8,128)(2,1)S(1)}, u32[]{:S(2)}, u32[]{:S(2)}) %all-to-all-start.2) | async-done | bytes 262176 | tf_op jit(solution)/shard_map/all_to_all | solution.py:79
  30.1 3.4 %all-to-all-start = ((bf16[256,4,128]{2,0,1:T(8,128)(2,1)}), bf16[256,4,128]{2,0,1:T(8,128)(2,1)S(1)}, u32[]{:S(2)}, u32[]{:S(2)}) async-start(bf16[256,4,128]{2,0,1:T(8,128)(2,1)} %copy.10), calls=%async_computation | async-start | bytes 524288 | tf_op jit(solution)/shard_map/all_to_all | solution.py:78
  33.5 0.2 convolution_bitcast_fusion
  33.8 0.2 convolution_bitcast_fusion.1
  34.0 5.5 %all-to-all-done = bf16[256,4,128]{2,0,1:T(8,128)(2,1)S(1)} async-done(((bf16[256,4,128]{2,0,1:T(8,128)(2,1)}), bf16[256,4,128]{2,0,1:T(8,128)(2,1)S(1)}, u32[]{:S(2)}, u32[]{:S(2)}) %all-to-all-start) | async-done | bytes 262176 | tf_op jit(solution)/shard_map/all_to_all | solution.py:78
  39.5 0.5 fusion.106
  40.0 0.7 convolution_convert_fusion.3
  40.7 1.3 %fusion.43 = f32[4,192,128]{2,1,0:T(8,128)} fusion(bf16[4,256,128]{2,1,0:T(8,128)(2,1)S(1)} %bitcast.71, f32[4,128]{1,0:T(4,128)S(1)} %get-tuple-element.74, bf16[4,256,128]{2,1,0:T(8,128)(2,1)S(1)} %bitcast.91, bf16[4,256,128]{2,1,0:T(8,128)(2,1)S(1)} %bitcast.83, bf16[3,64,128]{2,1,0:T(8,128)(2,1)S(1)} %slice.163, bf16[1,64,128]{2,1,0:T(8,128)(2,1)S(1)} %bitcast.105, ...), kind=kOutput, calls=%fused_computation.65 | convolution fusion | flops 53084864 | bytes 1040384 | tf_op jit(solution)/shard_map/dot_general | solution.py:63
  42.0 1.5 %fusion.103 = (f32[4,128]{1,0:T(4,128)S(1)}, f32[4,128,320]{1,2,0:T(8,128)}) fusion(bf16[4,256,128]{2,1,0:T(8,128)(2,1)S(1)} %bitcast.84, bf16[3,64,128]{2,1,0:T(8,128)(2,1)S(1)} %slice.163, bf16[1,64,128]{2,1,0:T(8,128)(2,1)S(1)} %bitcast.106, bf16[4,256,128]{2,1,0:T(8,128)(2,1)S(1)} %bitcast.92, pred[4]{0:T(512)(128)(4,1)S(1)} %add_compare_fusion, ...), kind=kOutput, calls=%fused_computation.111 | convolution fusion | flops 46367040 | bytes 1207296 | tf_op jit(solution)/shard_map/sub | solution.py:46
  43.6 0.9 %convolution_convert_fusion.2 = bf16[4,128,128]{2,1,0:T(8,128)(2,1)S(1)} fusion(bf16[4,256,128]{2,1,0:T(8,128)(2,1)S(1)} %bitcast.68, bf16[3,64,128]{2,1,0:T(8,128)(2,1)S(1)} %slice.166, bf16[1,64,128]{2,1,0:T(8,128)(2,1)S(1)} %bitcast.100, f32[4,128]{1,0:T(4,128)S(1)} %get-tuple-element.72, bf16[4,256,128]{2,1,0:T(8,128)(2,1)S(1)} %bitcast.85, ...), kind=kOutput, calls=%fused_computation.30 | convolution fusion | flops 89523008 | bytes 1010688 | tf_op jit(solution)/shard_map/dot_general | solution.py:49
  44.5 0.7 pad_maximum_fusion.4
  45.3 3.4 %all-to-all-start.1 = ((bf16[4,256,128]{2,1,0:T(8,128)(2,1)}), bf16[4,256,128]{2,1,0:T(8,128)(2,1)S(1)}, u32[]{:S(2)}, u32[]{:S(2)}) async-start(bf16[4,256,128]{2,1,0:T(8,128)(2,1)} %pad_maximum_fusion.4), calls=%async_computation.1 | async-start | bytes 524288 | tf_op jit(solution)/shard_map/all_to_all | solution.py:150
  48.7 1.7 %convolution_convert_fusion = bf16[4,128,128]{2,1,0:T(8,128)(2,1)S(1)} fusion(f32[4,128,320]{1,2,0:T(8,128)S(1)} %convolution_bitcast_fusion, bf16[4,256,128]{2,1,0:T(8,128)(2,1)S(1)} %bitcast.86, bf16[3,64,128]{2,1,0:T(8,128)(2,1)S(1)} %slice.163, bf16[1,64,128]{2,1,0:T(8,128)(2,1)S(1)} %bitcast.108, f32[4,128,320]{1,2,0:T(8,128)} %get-tuple-element.73, ...), kind=kOutput, calls=%fused_computation.28 | convolution fusion | flops 44139328 | bytes 1771520 | tf_op jit(solution)/shard_map/dot_general | solution.py:57
  50.4 1.0 %fusion.22 = f32[4,192,128]{2,1,0:T(8,128)} fusion(f32[4,128,192]{1,2,0:T(8,128)S(1)} %convolution_bitcast_fusion.1, bf16[4,256,128]{2,1,0:T(8,128)(2,1)S(1)} %bitcast.94, f32[4,128,192]{1,2,0:T(8,128)S(1)} %get-tuple-element.75, f32[4,128]{1,0:T(4,128)S(1)} %get-tuple-element.74), kind=kOutput, calls=%fused_computation.32 | convolution fusion | flops 25854656 | bytes 2101248 | tf_op jit(solution)/shard_map/dot_general | solution.py:60
  51.4 1.7 %convolution_add_fusion.1 = f32[4,320,128]{2,1,0:T(8,128)S(1)} fusion(f32[4,128,320]{1,2,0:T(8,128)S(1)} %convolution_bitcast_fusion, f32[4,192,128]{2,1,0:T(8,128)} %fusion.22, bf16[4,256,128]{2,1,0:T(8,128)(2,1)S(1)} %bitcast.95, f32[4,128,320]{1,2,0:T(8,128)} %get-tuple-element.73, f32[4,128]{1,0:T(4,128)S(1)} %get-tuple-element.72), kind=kOutput, calls=%fused_computation.11 | convolution fusion | flops 43254592 | bytes 3805184 | tf_op jit(solution)/shard_map/dot_general | solution.py:60
  53.2 3.3 %collective-permute-start.2 = (f32[64,128]{1,0:T(8,128)S(1)}, f32[64,128]{1,0:T(8,128)S(1)}, u32[]{:S(2)}, u32[]{:S(2)}) collective-permute-start(f32[64,128]{1,0:T(8,128)S(1)} %slice_bitcast_fusion.1), channel_id=1, source_target_pairs={{4,0},{8,4},{12,8},{16,12},{20,16},{24,20},{28,24},{5,1},{9,5},{13... | collective-permute-start | bytes 98312 | tf_op jit(solution)/shard_map/ppermute | solution.py:19
  56.6 1.9 %convolution_add_fusion = f32[4,320,128]{2,1,0:T(8,128)S(1)} fusion(f32[4,192,128]{2,1,0:T(8,128)} %fusion.43, bf16[4,256,128]{2,1,0:T(8,128)(2,1)S(1)} %bitcast.72, f32[4,128]{1,0:T(4,128)S(1)} %get-tuple-element.72, bf16[4,256,128]{2,1,0:T(8,128)(2,1)S(1)} %bitcast.87, bf16[3,64,128]{2,1,0:T(8,128)(2,1)S(1)} %copy-done.4, ...), kind=kOutput, calls=%fused_computation.10 | convolution fusion | flops 88638272 | bytes 1731584 | tf_op jit(solution)/shard_map/dot_general | solution.py:63
  58.4 0.4 convolution_convert_fusion.1
  58.8 0.7 pad_maximum_fusion.5
  59.6 3.4 %all-to-all-start.3 = ((bf16[4,256,128]{2,1,0:T(8,128)(2,1)}), bf16[4,256,128]{2,1,0:T(8,128)(2,1)S(1)}, u32[]{:S(2)}, u32[]{:S(2)}) async-start(bf16[4,256,128]{2,1,0:T(8,128)(2,1)} %pad_maximum_fusion.5), calls=%async_computation.3 | async-start | bytes 524288 | tf_op jit(solution)/shard_map/all_to_all | solution.py:151
  63.0 0.8 pad_maximum_fusion
  63.9 5.1 %all-to-all-done.3 = bf16[4,256,128]{2,1,0:T(8,128)(2,1)S(1)} async-done(((bf16[4,256,128]{2,1,0:T(8,128)(2,1)}), bf16[4,256,128]{2,1,0:T(8,128)(2,1)S(1)}, u32[]{:S(2)}, u32[]{:S(2)}) %all-to-all-start.3) | async-done | bytes 262176 | tf_op jit(solution)/shard_map/all_to_all | solution.py:151
  69.0 3.5 %all-to-all-start.4 = ((f32[4,256,128]{2,1,0:T(8,128)}), f32[4,256,128]{2,1,0:T(8,128)S(1)}, u32[]{:S(2)}, u32[]{:S(2)}) async-start(f32[4,256,128]{2,1,0:T(8,128)} %pad_maximum_fusion), calls=%async_computation.4 | async-start | bytes 1048576 | tf_op jit(solution)/shard_map/all_to_all | solution.py:154
  72.5 2.4 %collective-permute-start.3 = (f32[64,128]{1,0:T(8,128)S(1)}, f32[64,128]{1,0:T(8,128)S(1)}, u32[]{:S(2)}, u32[]{:S(2)}) collective-permute-start(f32[64,128]{1,0:T(8,128)S(1)} %slice_bitcast_fusion), channel_id=1, source_target_pairs={{4,0},{8,4},{12,8},{16,12},{20,16},{24,20},{28,24},{5,1},{9,5},{13... | collective-permute-start | bytes 98312 | tf_op jit(solution)/shard_map/ppermute | solution.py:19
  75.0 3.3 %collective-permute-done.3 = f32[64,128]{1,0:T(8,128)S(1)} collective-permute-done((f32[64,128]{1,0:T(8,128)S(1)}, f32[64,128]{1,0:T(8,128)S(1)}, u32[]{:S(2)}, u32[]{:S(2)}) %collective-permute-start.3) | collective-permute-done | bytes 32800 | tf_op jit(solution)/shard_map/ppermute | solution.py:19
  78.3 0.8 pad_maximum_fusion.1
  79.2 2.1 %all-to-all-done.4 = f32[4,256,128]{2,1,0:T(8,128)S(1)} async-done(((f32[4,256,128]{2,1,0:T(8,128)}), f32[4,256,128]{2,1,0:T(8,128)S(1)}, u32[]{:S(2)}, u32[]{:S(2)}) %all-to-all-start.4) | async-done | bytes 524320 | tf_op jit(solution)/shard_map/all_to_all | solution.py:154
  81.3 3.5 %all-to-all-start.5 = ((f32[4,256,128]{2,1,0:T(8,128)}), f32[4,256,128]{2,1,0:T(8,128)S(1)}, u32[]{:S(2)}, u32[]{:S(2)}) async-start(f32[4,256,128]{2,1,0:T(8,128)} %pad_maximum_fusion.1), calls=%async_computation.5 | async-start | bytes 1048576 | tf_op jit(solution)/shard_map/all_to_all | solution.py:155
  84.8 0.1 copy.11
  84.9 0.8 copy.15
  85.8 0.1 copy.14
  85.9 0.8 copy.16
  86.8 0.7 reduce_sum.58
  87.4 6.2 %all-to-all-done.5 = f32[4,256,128]{2,1,0:T(8,128)S(1)} async-done(((f32[4,256,128]{2,1,0:T(8,128)}), f32[4,256,128]{2,1,0:T(8,128)S(1)}, u32[]{:S(2)}, u32[]{:S(2)}) %all-to-all-start.5) | async-done | bytes 524320 | tf_op jit(solution)/shard_map/all_to_all | solution.py:155
  93.6 0.7 reduce_sum.59
  (49 shorter events, 0.3 us)
Async XLA Ops:
  0.6 9.7 %copy-start.2 = (bf16[256,128]{1,0:T(8,128)(2,1)S(1)}, bf16[256,128]{1,0:T(8,128)(2,1)}, u32[]{:S(2)}) copy-start(bf16[256,128]{1,0:T(8,128)(2,1)} %param.18) | copy-start | bytes 196612
  6.8 12.8 %copy-start = (bf16[256,512]{1,0:T(8,128)(2,1)S(1)}, bf16[256,512]{1,0:T(8,128)(2,1)}, u32[]{:S(2)}) copy-start(bf16[256,512]{1,0:T(8,128)(2,1)} %param.20) | copy-start | bytes 786436
  6.8 26.7 %collective-permute-start.1 = (bf16[64,128]{1,0:T(8,128)(2,1)S(1)}, bf16[64,128]{1,0:T(8,128)(2,1)S(1)}, u32[]{:S(2)}, u32[]{:S(2)}) collective-permute-start(bf16[64,128]{1,0:T(8,128)(2,1)S(1)} %slice_bitcast_fusion.2), channel_id=1, source_target_pairs={{0,4},{4,8},{8,12},{12,16},{16,20},{20,24},{24,28},{1,5},{5,9},{9,... | collective-permute-start | bytes 49160 | tf_op jit(solution)/shard_map/ppermute | solution.py:19
  16.1 17.9 %collective-permute-start = (bf16[64,128]{1,0:T(8,128)(2,1)S(1)}, bf16[64,128]{1,0:T(8,128)(2,1)S(1)}, u32[]{:S(2)}, u32[]{:S(2)}) collective-permute-start(bf16[64,128]{1,0:T(8,128)(2,1)S(1)} %slice_bitcast_fusion.3), channel_id=1, source_target_pairs={{0,4},{4,8},{8,12},{12,16},{16,20},{20,24},{24,28},{1,5},{5,9},{9,... | collective-permute-start | bytes 49160 | tf_op jit(solution)/shard_map/ppermute | solution.py:19
  20.5 3.7 %copy-start.8 = (s32[32]{0:T(128)S(1)}, s32[32]{0:T(128)}, u32[]{:S(2)}) copy-start(s32[32]{0:T(128)} %param.21) | copy-start | bytes 388
  20.6 9.5 %all-to-all-start.2 = ((bf16[256,4,128]{2,0,1:T(8,128)(2,1)}), bf16[256,4,128]{2,0,1:T(8,128)(2,1)S(1)}, u32[]{:S(2)}, u32[]{:S(2)}) async-start(bf16[256,4,128]{2,0,1:T(8,128)(2,1)} %copy.13), calls=%async_computation.2 | async-start | bytes 524288 | tf_op jit(solution)/shard_map/all_to_all | solution.py:79
  24.1 1.8 %copy-start.1 = (bf16[256,512]{1,0:T(8,128)(2,1)S(1)}, bf16[256,512]{1,0:T(8,128)(2,1)}, u32[]{:S(2)}) copy-start(bf16[256,512]{1,0:T(8,128)(2,1)} %param.17) | copy-start | bytes 786436
  24.1 19.4 %copy-start.11 = (pred[320]{0:T(512)(128)(4,1)}, pred[320]{0:T(512)(128)(4,1)S(1)}, u32[]{:S(2)}) copy-start(pred[320]{0:T(512)(128)(4,1)S(1)} %broadcast_compare_fusion.1) | copy-start | bytes 964
  24.2 19.4 %copy-start.9 = (pred[4]{0:T(512)(128)(4,1)}, pred[4]{0:T(512)(128)(4,1)S(1)}, u32[]{:S(2)}) copy-start(pred[4]{0:T(512)(128)(4,1)S(1)} %add_compare_fusion) | copy-start | bytes 16
  25.1 18.5 %copy-start.5 = (pred[128,320]{0,1:T(8,128)(4,1)}, pred[128,320]{0,1:T(8,128)(4,1)S(1)}, u32[]{:S(2)}) copy-start(pred[128,320]{0,1:T(8,128)(4,1)S(1)} %broadcast_compare_fusion) | copy-start | bytes 122884
  25.9 22.8 %copy-start.3 = (bf16[3,64,128]{2,1,0:T(8,128)(2,1)}, bf16[3,64,128]{2,1,0:T(8,128)(2,1)S(1)}, u32[]{:S(2)}) copy-start(bf16[3,64,128]{2,1,0:T(8,128)(2,1)S(1)} %slice.163) | copy-start | bytes 147460
  30.1 9.4 %all-to-all-start = ((bf16[256,4,128]{2,0,1:T(8,128)(2,1)}), bf16[256,4,128]{2,0,1:T(8,128)(2,1)S(1)}, u32[]{:S(2)}, u32[]{:S(2)}) async-start(bf16[256,4,128]{2,0,1:T(8,128)(2,1)} %copy.10), calls=%async_computation | async-start | bytes 524288 | tf_op jit(solution)/shard_map/all_to_all | solution.py:78
  34.0 14.7 %copy-start.6 = (bf16[64,128]{1,0:T(8,128)(2,1)}, bf16[64,128]{1,0:T(8,128)(2,1)S(1)}, u32[]{:S(2)}) copy-start(bf16[64,128]{1,0:T(8,128)(2,1)S(1)} %collective-permute-done) | copy-start | bytes 49156
  45.3 14.3 %all-to-all-start.1 = ((bf16[4,256,128]{2,1,0:T(8,128)(2,1)}), bf16[4,256,128]{2,1,0:T(8,128)(2,1)S(1)}, u32[]{:S(2)}, u32[]{:S(2)}) async-start(bf16[4,256,128]{2,1,0:T(8,128)(2,1)} %pad_maximum_fusion.4), calls=%async_computation.1 | async-start | bytes 524288 | tf_op jit(solution)/shard_map/all_to_all | solution.py:150
  51.4 5.1 %copy-start.10 = (pred[4]{0:T(512)(128)(4,1)S(1)}, pred[4]{0:T(512)(128)(4,1)}, u32[]{:S(2)}) copy-start(pred[4]{0:T(512)(128)(4,1)} %copy-done.9) | copy-start | bytes 16
  51.4 5.1 %copy-start.12 = (pred[320]{0:T(512)(128)(4,1)S(1)}, pred[320]{0:T(512)(128)(4,1)}, u32[]{:S(2)}) copy-start(pred[320]{0:T(512)(128)(4,1)} %copy-done.11) | copy-start | bytes 964
  53.2 3.4 %copy-start.4 = (bf16[3,64,128]{2,1,0:T(8,128)(2,1)S(1)}, bf16[3,64,128]{2,1,0:T(8,128)(2,1)}, u32[]{:S(2)}) copy-start(bf16[3,64,128]{2,1,0:T(8,128)(2,1)} %copy-done.3) | copy-start | bytes 147460
  53.2 3.4 %copy-start.7 = (bf16[64,128]{1,0:T(8,128)(2,1)S(1)}, bf16[64,128]{1,0:T(8,128)(2,1)}, u32[]{:S(2)}) copy-start(bf16[64,128]{1,0:T(8,128)(2,1)} %copy-done.6) | copy-start | bytes 49156
  53.2 9.8 %collective-permute-start.2 = (f32[64,128]{1,0:T(8,128)S(1)}, f32[64,128]{1,0:T(8,128)S(1)}, u32[]{:S(2)}, u32[]{:S(2)}) collective-permute-start(f32[64,128]{1,0:T(8,128)S(1)} %slice_bitcast_fusion.1), channel_id=1, source_target_pairs={{4,0},{8,4},{12,8},{16,12},{20,16},{24,20},{28,24},{5,1},{9,5},{13... | collective-permute-start | bytes 98312 | tf_op jit(solution)/shard_map/ppermute | solution.py:19
  59.6 9.4 %all-to-all-start.3 = ((bf16[4,256,128]{2,1,0:T(8,128)(2,1)}), bf16[4,256,128]{2,1,0:T(8,128)(2,1)S(1)}, u32[]{:S(2)}, u32[]{:S(2)}) async-start(bf16[4,256,128]{2,1,0:T(8,128)(2,1)} %pad_maximum_fusion.5), calls=%async_computation.3 | async-start | bytes 524288 | tf_op jit(solution)/shard_map/all_to_all | solution.py:151
  69.0 12.3 %all-to-all-start.4 = ((f32[4,256,128]{2,1,0:T(8,128)}), f32[4,256,128]{2,1,0:T(8,128)S(1)}, u32[]{:S(2)}, u32[]{:S(2)}) async-start(f32[4,256,128]{2,1,0:T(8,128)} %pad_maximum_fusion), calls=%async_computation.4 | async-start | bytes 1048576 | tf_op jit(solution)/shard_map/all_to_all | solution.py:154
  72.5 5.8 %collective-permute-start.3 = (f32[64,128]{1,0:T(8,128)S(1)}, f32[64,128]{1,0:T(8,128)S(1)}, u32[]{:S(2)}, u32[]{:S(2)}) collective-permute-start(f32[64,128]{1,0:T(8,128)S(1)} %slice_bitcast_fusion), channel_id=1, source_target_pairs={{4,0},{8,4},{12,8},{16,12},{20,16},{24,20},{28,24},{5,1},{9,5},{13... | collective-permute-start | bytes 98312 | tf_op jit(solution)/shard_map/ppermute | solution.py:19
  81.3 12.3 %all-to-all-start.5 = ((f32[4,256,128]{2,1,0:T(8,128)}), f32[4,256,128]{2,1,0:T(8,128)S(1)}, u32[]{:S(2)}, u32[]{:S(2)}) async-start(f32[4,256,128]{2,1,0:T(8,128)} %pad_maximum_fusion.1), calls=%async_computation.5 | async-start | bytes 1048576 | tf_op jit(solution)/shard_map/all_to_all | solution.py:155
where the time goes:
time: 95.1 us; the launch traced here: 94.2 us
  starting transfers between devices  33.4 us (35%)
  waiting for transfers between devices  25.5 us (27%)
  matrix products  12.1 us (13%)
  blocking collectives  11.9 us (13%)
  other arithmetic  5.42 us (6%)
  local copies, waits for them, and re-layouts  4.74 us (5%)
  between operations  1.09 us (1%)
    ppermute x4, starting transfers between devices, passed_along(): lax.ppermute(value, axis, [(source, source + steps) for source in range(f...  12.7 us
    all_to_all x1, waiting for transfers between devices, per_device(): lax.all_to_all(own_v, 'head', split_axis=0, concat_axis=1, tiled=True)  6.16 us
    all_gather x1, blocking collectives, per_device(): lax.all_gather(value_rows, 'head', axis=0, tiled=True)  6.13 us
    all_gather x1, blocking collectives, per_device(): lax.all_gather(key_rows, 'head', axis=0, tiled=True)  5.79 us
    all_to_all x1, waiting for transfers between devices, per_device(): lax.all_to_all(queries, 'head', split_axis=1, concat_axis=0, tiled=True)  5.5 us
    all_to_all x1, waiting for transfers between devices, per_device(): lax.all_to_all(all_query_grads, 'head', split_axis=0, concat_axis=1, tile...  5.14 us
    all_to_all x1, starting transfers between devices, per_device(): lax.all_to_all(out_grad, 'head', split_axis=1, concat_axis=0, tiled=True)  3.54 us
    all_to_all x1, starting transfers between devices, per_device(): lax.all_to_all(own_k, 'head', split_axis=0, concat_axis=1, tiled=True)  3.47 us
  transfers between devices with their start and end apart: 10, of which 6 were waited for; matrix products, arithmetic and copies ran while one was open for 17% of the time, Pallas kernels for 0%

commit v1 on v0

--- a/solution.py
+++ b/solution.py
@@ -3,11 +3,15 @@
 import jax
 import jax.numpy as jnp
 from jax import lax
+from jax.experimental import pallas as pl
+from jax.experimental.pallas import tpu as pltpu
 from jax.sharding import PartitionSpec as P
 
 HD = 128
 GROUP = 4
 SPANS_DEV = 4
+SCALE = 1.0 / math.sqrt(HD)
+LOG2_SCALE = SCALE * math.log2(math.e)
 
 
 masked_fill = -1e30
@@ -66,7 +70,7 @@
     return (result, grad_query, grad_key, grad_value)
 
 
-def per_device(queries, key_rows, value_rows, out_grad, doc_start):
+def spans_over_devices(queries, key_rows, value_rows, out_grad, doc_start):
     tok_count = queries.shape[0]
     head_count = lax.axis_size("head")
     group_rows = tok_count * head_count
@@ -170,6 +174,205 @@
     return (outputs, query_grad, key_grad, value_grad)
 
 
+ROWS_BY_ROWS = (((1,), (1,)), ((), ()))
+COLS_BY_COLS = (((0,), (0,)), ((), ()))
+PLAIN = (((1,), (0,)), ((), ()))
+
+
+def dot(left, right, dims):
+    return lax.dot_general(left, right, dims, preferred_element_type=jnp.float32)
+
+
+def head_cols(head):
+    return slice(head * HD, (head + 1) * HD)
+
+
+def own_kernel(span, halo, doc_ref, q_ref, g_ref, k_ref, v_ref, exp_ref, gw_ref, stat_ref, mask_ref):
+    device = lax.axis_index("seq") * lax.axis_size("head") + lax.axis_index("head")
+    start = doc_ref[device]
+    before = doc_ref[jnp.maximum(device - 1, 0)]
+    key_pos = lax.broadcasted_iota(jnp.int32, (span, span), 0)
+    row_pos = lax.broadcasted_iota(jnp.int32, (span, span), 1)
+    allowed = (key_pos <= row_pos) & ((key_pos >= start) | (start > row_pos))
+    halo_pos = lax.broadcasted_iota(jnp.int32, (halo, span), 0) - halo
+    halo_row = lax.broadcasted_iota(jnp.int32, (halo, span), 1)
+    first = jnp.where(device > 0, before - span, span)
+    halo_ok = ((halo_pos >= start) | (start > halo_row)) & (halo_pos >= first)
+    mask_ref[...] = jnp.where(halo_ok, 0.0, masked_fill)
+    keys = k_ref[...]
+    values = v_ref[...]
+    for head in range(GROUP):
+        scores = dot(keys, q_ref[:, head_cols(head)], ROWS_BY_ROWS) * LOG2_SCALE
+        scores = jnp.where(allowed, scores, masked_fill)
+        top = jnp.max(scores, axis=0, keepdims=True)
+        weights = jnp.exp2(scores - top)
+        grad_weights = dot(values, g_ref[:, head_cols(head)], ROWS_BY_ROWS)
+        exp_ref[head * span : (head + 1) * span] = weights
+        gw_ref[head * span : (head + 1) * span] = grad_weights
+        stat_ref[head : head + 1] = top
+        stat_ref[GROUP + head : GROUP + head + 1] = jnp.sum(weights, axis=0, keepdims=True)
+        stat_ref[2 * GROUP + head : 2 * GROUP + head + 1] = jnp.sum(
+            weights * grad_weights, axis=0, keepdims=True
+        )
+
+
+def halo_kernel(halo, mask_ref, edge_ref, q_ref, g_ref, stat_ref, p_ref, ds_ref, row_ref, back_ref):
+    keys = edge_ref[:, :HD]
+    values = edge_ref[:, HD:]
+    mask = mask_ref[...]
+    grad_key = jnp.zeros((halo, HD), jnp.float32)
+    grad_value = jnp.zeros((halo, HD), jnp.float32)
+    for head in range(GROUP):
+        queries = q_ref[:, head_cols(head)]
+        grads = g_ref[:, head_cols(head)]
+        scores = dot(keys, queries, ROWS_BY_ROWS) * LOG2_SCALE + mask
+        grad_weights = dot(values, grads, ROWS_BY_ROWS)
+        own_top = stat_ref[head : head + 1]
+        top = jnp.maximum(jnp.max(scores, axis=0, keepdims=True), own_top)
+        weights = jnp.exp2(scores - top)
+        shift = jnp.exp2(own_top - top)
+        total = stat_ref[GROUP + head : GROUP + head + 1] * shift + jnp.sum(weights, axis=0, keepdims=True)
+        inner = stat_ref[2 * GROUP + head : 2 * GROUP + head + 1] * shift + jnp.sum(
+            weights * grad_weights, axis=0, keepdims=True
+        )
+        delta = inner / total
+        p = weights / total
+        p_low = p.astype(jnp.bfloat16)
+        ds_low = (p * (grad_weights - delta) * SCALE).astype(jnp.bfloat16)
+        grad_key += dot(ds_low, queries, PLAIN)
+        grad_value += dot(p_low, grads, PLAIN)
+        p_ref[head * halo : (head + 1) * halo] = p_low
+        ds_ref[head * halo : (head + 1) * halo] = ds_low
+        row_ref[head : head + 1] = shift / total
+        row_ref[GROUP + head : GROUP + head + 1] = delta
+    back_ref[:, :HD] = grad_key.astype(back_ref.dtype)
+    back_ref[:, HD:] = grad_value.astype(back_ref.dtype)
+
+
+def rest_kernel(
+    span, halo, q_ref, g_ref, k_ref, v_ref, edge_ref, exp_ref, gw_ref, p_ref, ds_ref, row_ref,
+    out_ref, dq_ref, dk_ref, dv_ref, tail_ref,
+):
+    keys = k_ref[...]
+    values = v_ref[...]
+    edge_keys = edge_ref[:, :HD]
+    edge_values = edge_ref[:, HD:]
+    grad_key = jnp.zeros((span, HD), jnp.float32)
+    grad_value = jnp.zeros((span, HD), jnp.float32)
+    for head in range(GROUP):
+        queries = q_ref[:, head_cols(head)]
+        grads = g_ref[:, head_cols(head)]
+        p = exp_ref[head * span : (head + 1) * span] * row_ref[head : head + 1]
+        p_low = p.astype(jnp.bfloat16)
+        inner = gw_ref[head * span : (head + 1) * span] - row_ref[GROUP + head : GROUP + head + 1]
+        ds_low = (p * inner * SCALE).astype(jnp.bfloat16)
+        p_edge = p_ref[head * halo : (head + 1) * halo]
+        ds_edge = ds_ref[head * halo : (head + 1) * halo]
+        out = dot(p_low, values, COLS_BY_COLS) + dot(p_edge, edge_values, COLS_BY_COLS)
+        out_ref[:, head_cols(head)] = out.astype(jnp.bfloat16)
+        dq = dot(ds_low, keys, COLS_BY_COLS) + dot(ds_edge, edge_keys, COLS_BY_COLS)
+        dq_ref[:, head_cols(head)] = dq.astype(jnp.bfloat16)
+        grad_key += dot(ds_low, queries, PLAIN)
+        grad_value += dot(p_low, grads, PLAIN)
+    dk_ref[...] = grad_key.astype(jnp.bfloat16)
+    dv_ref[...] = grad_value.astype(jnp.bfloat16)
+    tail_ref[:, :HD] = grad_key[span - halo :]
+    tail_ref[:, HD:] = grad_value[span - halo :]
+
+
+def tail_kernel(span, halo, tail_ref, back_ref, dk_in, dv_in, dk_ref, dv_ref, sum_ref, sems):
+    del dk_in, dv_in
+    total = tail_ref[...] + back_ref[...].astype(jnp.float32)
+    sum_ref[0] = total[:, :HD].astype(jnp.bfloat16)
+    sum_ref[1] = total[:, HD:].astype(jnp.bfloat16)
+    copies = [
+        pltpu.make_async_copy(sum_ref.at[at], ref.at[pl.ds(span - halo, halo)], sems.at[at])
+        for at, ref in enumerate((dk_ref, dv_ref))
+    ]
+    for copy in copies:
+        copy.start()
+    for copy in copies:
+        copy.wait()
+
+
+def passed_on(value, steps):
+    axes = ("seq", "head")
+    count = lax.axis_size("seq") * lax.axis_size("head")
+    first, last = (max(0, -steps), min(count, count - steps))
+    return lax.ppermute(value, axes, [(source, source + steps) for source in range(first, last)])
+
+
+def span_on_device(queries, key_rows, value_rows, out_grad, doc_start):
+    span = queries.shape[0]
+    halo = span // 4
+    vmem = pl.BlockSpec(memory_space=pltpu.VMEM)
+    smem = pl.BlockSpec(memory_space=pltpu.SMEM)
+    hbm = pl.BlockSpec(memory_space=pl.ANY)
+    f32, bf16 = (jnp.float32, jnp.bfloat16)
+    near = lambda value: pltpu.with_memory_space_constraint(value, pltpu.VMEM)
+    edge = passed_on(
+        jnp.concatenate([key_rows[span - halo :], value_rows[span - halo :]], axis=1), 1
+    )
+    exp_own, gw_own, stats, mask = pl.pallas_call(
+        lambda *refs: own_kernel(span, halo, *refs),
+        in_specs=[smem, vmem, vmem, vmem, vmem],
+        out_specs=[vmem] * 4,
+        out_shape=[
+            pltpu.VMEM((GROUP * span, span), f32),
+            pltpu.VMEM((GROUP * span, span), f32),
+            pltpu.VMEM((4 * GROUP, span), f32),
+            pltpu.VMEM((halo, span), f32),
+        ],
+        name="own_scores",
+    )(doc_start, near(queries), near(out_grad), near(key_rows), near(value_rows))
+    p_edge, ds_edge, rows, back = pl.pallas_call(
+        lambda *refs: halo_kernel(halo, *refs),
+        in_specs=[vmem] * 5,
+        out_specs=[vmem] * 4,
+        out_shape=[
+            pltpu.VMEM((GROUP * halo, span), bf16),
+            pltpu.VMEM((GROUP * halo, span), bf16),
+            pltpu.VMEM((2 * GROUP, span), f32),
+            pltpu.VMEM((halo, 2 * HD), f32),
+        ],
+        name="halo_grads",
+    )(near(mask), near(edge), near(queries), near(out_grad), near(stats))
+    returned = passed_on(back, -1)
+    outputs, query_grad, key_grad, value_grad, tail = pl.pallas_call(
+        lambda *refs: rest_kernel(span, halo, *refs),
+        in_specs=[vmem] * 10,
+        out_specs=[vmem] * 5,
+        out_shape=[
+            jax.ShapeDtypeStruct(queries.shape, bf16),
+            jax.ShapeDtypeStruct(queries.shape, bf16),
+            jax.ShapeDtypeStruct(key_rows.shape, bf16),
+            jax.ShapeDtypeStruct(key_rows.shape, bf16),
+            pltpu.VMEM((halo, 2 * HD), f32),
+        ],
+        name="own_grads",
+    )(*[near(x) for x in (queries, out_grad, key_rows, value_rows, edge, exp_own, gw_own, p_edge, ds_edge, rows)])
+    key_grad, value_grad = pl.pallas_call(
+        lambda *refs: tail_kernel(span, halo, *refs),
+        in_specs=[vmem, vmem, hbm, hbm],
+        out_specs=[hbm, hbm],
+        out_shape=[
+            jax.ShapeDtypeStruct(key_rows.shape, bf16),
+            jax.ShapeDtypeStruct(key_rows.shape, bf16),
+        ],
+        scratch_shapes=[pltpu.VMEM((2, halo, HD), bf16), pltpu.SemaphoreType.DMA((2,))],
+        input_output_aliases={2: 0, 3: 1},
+        name="tail_grads",
+    )(near(tail), near(returned), key_grad, value_grad)
+    return (outputs, query_grad, key_grad, value_grad)
+
+
+def per_device(queries, key_rows, value_rows, out_grad, doc_start):
+    span = queries.shape[0] * lax.axis_size("head") // SPANS_DEV
+    whole_span = span == queries.shape[0] and key_rows.shape[1] == HD and queries.shape[1] == GROUP * HD
+    plan = span_on_device if whole_span else spans_over_devices
+    return plan(queries, key_rows, value_rows, out_grad, doc_start)
+
+
 def solution(mesh):
     placed = (
         P(("seq", "head"), None),

time: 95.1 us -> 19.2 us (0.20)
  the two profiles are of different devices: /device:TPU:8 before, /device:TPU:7 now
where the time goes in v1:
time: 19.2 us; the launch traced here: 18.9 us
  local copies, waits for them, and re-layouts  5.64 us (29%)
  starting transfers between devices  5.59 us (29%)
  Pallas kernels  4.39 us (23%)
  waiting for transfers between devices  2.53 us (13%)
  between operations  0.72 us (4%)
    ppermute x2, starting transfers between devices, passed_on(): lax.ppermute(value, axes, [(source, source + steps) for source in range(f...  5.59 us
    unnamed x14, local copies, waits for them, and re-layouts  4.93 us
    ppermute x2, waiting for transfers between devices, passed_on(): lax.ppermute(value, axes, [(source, source + steps) for source in range(f...  2.53 us
    pallas_call x1, Pallas kernels, span_on_device(): pl.pallas_call(lambda *refs: rest_kernel(span, halo, *refs), in_specs=[vm...  1.69 us
    pallas_call x1, Pallas kernels, span_on_device(): pl.pallas_call(lambda *refs: own_kernel(span, halo, *refs), in_specs=[sme...  1.2 us
    pallas_call x1, Pallas kernels, span_on_device(): pl.pallas_call(lambda *refs: halo_kernel(halo, *refs), in_specs=[vmem] *...  0.87 us
    slice x2, local copies, waits for them, and re-layouts, span_on_device(): value_rows[span - halo:]  0.69 us
    pallas_call x1, Pallas kernels, span_on_device(): pl.pallas_call(lambda *refs: tail_kernel(span, halo, *refs), in_specs=[vm...  0.64 us
  transfers between devices with their start and end apart: 2, of which 1 were waited for; matrix products, arithmetic and copies ran while one was open for 0% of the time, Pallas kernels for 15%

profile of v1, /device:TPU:7, one launch (start us, length us, event | category | flops | bytes accessed | tf_op | source)
XLA Modules:
  0.0 18.9 jit_solution(7133936702683418145)
XLA Ops:
  0.6 0.0 slice-start.1
  0.6 0.0 slice-start
  0.7 0.0 copy-start.4
  0.7 0.7 %slice-done.1 = bf16[64,128]{1,0:T(8,128)(2,1)S(1)} async-done(((bf16[256,128]{1,0:T(8,128)(2,1)}), bf16[64,128]{1,0:T(8,128)(2,1)S(1)}, s32[]{:S(2)}) %slice-start.1) | async-done | bytes 16408 | tf_op jit(solution)/shard_map/slice | solution.py:314
  1.4 0.0 slice-done
  1.4 3.7 %collective-permute-start = (bf16[64,256]{1,0:T(8,128)(2,1)S(1)}, bf16[64,256]{1,0:T(8,128)(2,1)S(1)}, u32[]{:S(2)}, u32[]{:S(2)}) collective-permute-start(bf16[64,256]{1,0:T(8,128)(2,1)S(1)} %pad_maximum_fusion), channel_id=1, source_target_pairs={{0,1},{1,2},{2,3},{3,4},{4,5},{5,6},{6,7},{7,8},{8,9},{9,10},{10,1... | collective-permute-start | bytes 98312 | tf_op jit(solution)/shard_map/ppermute | solution.py:302
  5.1 0.0 copy-done.4
  5.1 0.0 copy-start
  5.1 0.9 %copy-done = bf16[256,512]{1,0:T(8,128)(2,1)S(1)} copy-done((bf16[256,512]{1,0:T(8,128)(2,1)S(1)}, bf16[256,512]{1,0:T(8,128)(2,1)}, u32[]{:S(2)}) %copy-start) | copy-done | bytes 262168
  6.0 0.0 copy-start.1
  6.0 0.9 %copy-done.1 = bf16[256,512]{1,0:T(8,128)(2,1)S(1)} copy-done((bf16[256,512]{1,0:T(8,128)(2,1)S(1)}, bf16[256,512]{1,0:T(8,128)(2,1)}, u32[]{:S(2)}) %copy-start.1) | copy-done | bytes 262168
  7.0 0.0 copy-start.5
  7.0 0.8 %copy-done.5 = bf16[256,128]{1,0:T(8,128)(2,1)S(1)} copy-done((bf16[256,128]{1,0:T(8,128)(2,1)S(1)}, bf16[256,128]{1,0:T(8,128)(2,1)}, u32[]{:S(2)}) %copy-start.5) | copy-done | bytes 65560
  7.8 1.2 %own_scores.1 = (f32[1024,256]{1,0:T(8,128)S(1)}, f32[1024,256]{1,0:T(8,128)S(1)}, f32[16,256]{1,0:T(8,128)S(1)}, f32[64,256]{1,0:T(8,128)S(1)}) custom-call(s32[32]{0:T(128)} %refs_0_.2, bf16[256,512]{1,0:T(8,128)(2,1)S(1)} %copy-done, bf16[256,512]{1,0:T(8,128)(2,1)S(1)} %copy-done.1, bf16[256,128]{1,0:T(8,128)(2,1)S(1)} %copy-done.4, ...), custom_call_target="tpu_custom_call" | custom-call | tf_op jit(solution)/shard_map/own_scores/pallas_call | solution.py:316
  9.0 0.0 copy-start.2
  9.0 1.0 %copy-done.2 = f32[1024,256]{1,0:T(8,128)} copy-done((f32[1024,256]{1,0:T(8,128)}, f32[1024,256]{1,0:T(8,128)S(1)}, u32[]{:S(2)}) %copy-start.2) | copy-done | bytes 1048600
  10.0 0.0 collective-permute-done.refs_1_.refs_4_
  10.0 0.0 copy-start.6
  10.0 0.9 %halo_grads.1 = (bf16[256,256]{1,0:T(8,128)(2,1)S(1)}, bf16[256,256]{1,0:T(8,128)(2,1)S(1)}, f32[8,256]{1,0:T(8,128)S(1)}, f32[64,256]{1,0:T(8,128)S(1)}) custom-call(f32[64,256]{1,0:T(8,128)S(1)} %get-tuple-element.21.refs_0_, bf16[64,256]{1,0:T(8,128)(2,1)S(1)} %collective-permute-done.refs_1_.refs_4_, bf16[256,512]{1,0:T(8,128)(2,1)S(1)} %copy-done, ...), custom_call_target="tpu_custom_call" | custom-call | tf_op jit(solution)/shard_map/halo_grads/pallas_call | solution.py:328
  10.9 1.9 %collective-permute-start.1 = (f32[64,256]{1,0:T(8,128)S(1)}, f32[64,256]{1,0:T(8,128)S(1)}, u32[]{:S(2)}, u32[]{:S(2)}) collective-permute-start(f32[64,256]{1,0:T(8,128)S(1)} %get-tuple-element.29), channel_id=1, source_target_pairs={{1,0},{2,1},{3,2},{4,3},{5,4},{6,5},{7,6},{8,7},{9,8},{10,9},{11,1... | collective-permute-start | bytes 196616 | tf_op jit(solution)/shard_map/ppermute | solution.py:302
  12.8 0.0 copy-done.6
  12.8 0.0 copy-start.3
  12.8 1.2 %copy-done.3 = f32[1024,256]{1,0:T(8,128)S(1)} copy-done((f32[1024,256]{1,0:T(8,128)S(1)}, f32[1024,256]{1,0:T(8,128)}, u32[]{:S(2)}) %copy-start.3) | copy-done | bytes 1048600
  14.0 1.7 %own_grads.1 = (bf16[256,512]{1,0:T(8,128)(2,1)}, bf16[256,512]{1,0:T(8,128)(2,1)}, bf16[256,128]{1,0:T(8,128)(2,1)}, bf16[256,128]{1,0:T(8,128)(2,1)}, f32[64,256]{1,0:T(8,128)S(1)}) custom-call(bf16[256,512]{1,0:T(8,128)(2,1)S(1)} %copy-done, bf16[256,512]{1,0:T(8,128)(2,1)S(1)} %copy-done.1, bf16[256,128]{1,0:T(8,128)(2,1)S(1)} %copy-done.4, ...), custom_call_target="tpu_custom_call" | custom-call | tf_op jit(solution)/shard_map/own_grads/pallas_call | solution.py:341
  15.7 2.5 %collective-permute-done.1.refs_1_ = f32[64,256]{1,0:T(8,128)S(1)} collective-permute-done((f32[64,256]{1,0:T(8,128)S(1)}, f32[64,256]{1,0:T(8,128)S(1)}, u32[]{:S(2)}, u32[]{:S(2)}) %collective-permute-start.1) | collective-permute-done | bytes 65568 | tf_op jit(solution)/shard_map/ppermute | solution.py:302
  18.3 0.6 %tail_grads.1 = (bf16[256,128]{1,0:T(8,128)(2,1)}, bf16[256,128]{1,0:T(8,128)(2,1)}) custom-call(f32[64,256]{1,0:T(8,128)S(1)} %get-tuple-element.28.refs_0_, f32[64,256]{1,0:T(8,128)S(1)} %collective-permute-done.1.refs_1_, bf16[256,128]{1,0:T(8,128)(2,1)} %get-tuple-element.30.refs_2_, ...), custom_call_target="tpu_custom_call", output_to_operand_aliasing={{0}: (2, {}), {1}: (3, {})} | custom-call | tf_op jit(solution)/shard_map/tail_grads/pallas_call | solution.py:354
  (1 shorter events, 0.0 us)
Async XLA Ops:
  0.6 0.7 %slice-start.1 = ((bf16[256,128]{1,0:T(8,128)(2,1)}), bf16[64,128]{1,0:T(8,128)(2,1)S(1)}, s32[]{:S(2)}) async-start(bf16[256,128]{1,0:T(8,128)(2,1)} %refs_3_.5), calls=%async_computation.1 | async-start | bytes 32768 | tf_op jit(solution)/shard_map/slice | solution.py:314
  0.6 0.7 %slice-start = ((bf16[256,128]{1,0:T(8,128)(2,1)}), bf16[64,128]{1,0:T(8,128)(2,1)S(1)}, s32[]{:S(2)}) async-start(bf16[256,128]{1,0:T(8,128)(2,1)} %refs_2_.5), calls=%async_computation | async-start | bytes 32768 | tf_op jit(solution)/shard_map/slice | solution.py:314
  0.7 4.4 %copy-start.4 = (bf16[256,128]{1,0:T(8,128)(2,1)S(1)}, bf16[256,128]{1,0:T(8,128)(2,1)}, u32[]{:S(2)}) copy-start(bf16[256,128]{1,0:T(8,128)(2,1)} %refs_2_.5) | copy-start | bytes 196612
  1.4 8.6 %collective-permute-start = (bf16[64,256]{1,0:T(8,128)(2,1)S(1)}, bf16[64,256]{1,0:T(8,128)(2,1)S(1)}, u32[]{:S(2)}, u32[]{:S(2)}) collective-permute-start(bf16[64,256]{1,0:T(8,128)(2,1)S(1)} %pad_maximum_fusion), channel_id=1, source_target_pairs={{0,1},{1,2},{2,3},{3,4},{4,5},{5,6},{6,7},{7,8},{8,9},{9,10},{10,1... | collective-permute-start | bytes 98312 | tf_op jit(solution)/shard_map/ppermute | solution.py:302
  5.1 1.0 %copy-start = (bf16[256,512]{1,0:T(8,128)(2,1)S(1)}, bf16[256,512]{1,0:T(8,128)(2,1)}, u32[]{:S(2)}) copy-start(bf16[256,512]{1,0:T(8,128)(2,1)} %refs_0_.3) | copy-start | bytes 786436
  6.0 0.9 %copy-start.1 = (bf16[256,512]{1,0:T(8,128)(2,1)S(1)}, bf16[256,512]{1,0:T(8,128)(2,1)}, u32[]{:S(2)}) copy-start(bf16[256,512]{1,0:T(8,128)(2,1)} %refs_1_.3) | copy-start | bytes 786436
  7.0 0.8 %copy-start.5 = (bf16[256,128]{1,0:T(8,128)(2,1)S(1)}, bf16[256,128]{1,0:T(8,128)(2,1)}, u32[]{:S(2)}) copy-start(bf16[256,128]{1,0:T(8,128)(2,1)} %refs_3_.5) | copy-start | bytes 196612
  9.0 1.0 %copy-start.2 = (f32[1024,256]{1,0:T(8,128)}, f32[1024,256]{1,0:T(8,128)S(1)}, u32[]{:S(2)}) copy-start(f32[1024,256]{1,0:T(8,128)S(1)} %get-tuple-element.19.refs_5_) | copy-start | bytes 3145732
  10.0 2.8 %copy-start.6 = (bf16[256,128]{1,0:T(8,128)(2,1)S(1)}, bf16[256,128]{1,0:T(8,128)(2,1)}, u32[]{:S(2)}) copy-start(bf16[256,128]{1,0:T(8,128)(2,1)} %refs_3_.5) | copy-start | bytes 196612
  10.9 7.4 %collective-permute-start.1 = (f32[64,256]{1,0:T(8,128)S(1)}, f32[64,256]{1,0:T(8,128)S(1)}, u32[]{:S(2)}, u32[]{:S(2)}) collective-permute-start(f32[64,256]{1,0:T(8,128)S(1)} %get-tuple-element.29), channel_id=1, source_target_pairs={{1,0},{2,1},{3,2},{4,3},{5,4},{6,5},{7,6},{8,7},{9,8},{10,9},{11,1... | collective-permute-start | bytes 196616 | tf_op jit(solution)/shard_map/ppermute | solution.py:302
  12.8 1.2 %copy-start.3 = (f32[1024,256]{1,0:T(8,128)S(1)}, f32[1024,256]{1,0:T(8,128)}, u32[]{:S(2)}) copy-start(f32[1024,256]{1,0:T(8,128)} %copy-done.2) | copy-start | bytes 3145732
